TPU v7x, 256 devices: a whole 4x4x8 slice. The times are simulated.
256 devices in a mesh: param: 64 (over x, z, core), ex: 4 (over y).
Axes of the slice: x: 4, y: 4, z: 8, core: 2. Of those that a mesh axis runs over, the one named last changes fastest.
Arguments:
- gradients: float32 [256, 262144], P('ex', 'param')
- m_state: float32 [262144], P('param'), may hold values from -0.6 to 0.6
- v_state: float32 [262144], P('param'), may hold values from 0.001 to 0.1
- row_seeds: int32 [262144], P('param'), may hold values from 1 to 2999999
- col_seeds: int32 [8192], replicated, may hold values from 1 to 2999999
- group_of: int32 [256], replicated, may hold values from 0 to 56, as said below
Outputs:
- features: float32 [256, 8192], P('ex', 'param')
- scores: float32 [256, 57], P('ex')
Inputs may be any that keep to these rules, and one draw needn't show every extreme that they name: `group_of`: every one of the 57 subtasks holds at least one example.
All inputs are finite; a program needn't handle non-finite values.
Results may differ from a plain program's by a relative error of at most 0.0029.
Values sent between devices are 32-bit elements; how exact they have to be, the bound alone decides.
A program may use at most 64 MiB of HBM per device.

v0:
```python
import jax
import jax.numpy as jnp
from jax import lax
from jax.sharding import PartitionSpec as P

GROUPS = 57


def in_blocks(value, dim, count):
    before, after = (value.shape[:dim], value.shape[dim + 1 :])
    return jnp.moveaxis(value.reshape(*before, count, -1, *after), dim, 0)


def summed_on_arrival(value, axis, dim):
    count = lax.axis_size(axis)
    pieces = lax.all_to_all(in_blocks(value, dim, count), axis, 0, 0, tiled=True)
    return jnp.sum(pieces, axis=0)


def from_everyone(value, axis):
    copies = jnp.broadcast_to(value, (lax.axis_size(axis), *value.shape))
    return lax.all_to_all(copies, axis, split_axis=0, concat_axis=0, tiled=True)


def of_everyone(value, axis):
    return from_everyone(value, axis).sum(axis=0)


def laid_out(pieces, dim):
    dims = list(pieces.shape[1:])
    dims[dim] *= pieces.shape[0]
    return jnp.moveaxis(pieces, 0, dim).reshape(dims)


def collect(value, axis, dim):
    return laid_out(from_everyone(value, axis), dim)


def hashed_signs(row_part, col_part):
    hashed = row_part[:, None] * col_part[None, :]
    hashed = hashed ^ hashed >> 15
    hashed = hashed * jnp.int32(739982445)
    hashed = hashed ^ hashed >> 13
    return (1 - 2 * (hashed >> 11 & 1)).astype(jnp.bfloat16)


def shards(gradients, m_state, v_state, row_seeds, col_seeds, group_of):
    first_moment = 0.9 * m_state[None, :] + 0.1 * gradients
    second_moment = 0.999 * v_state[None, :] + 0.001 * gradients * gradients
    update = (first_moment / (jnp.sqrt(second_moment) + 1e-08)).astype(jnp.bfloat16)
    examples_here = update.shape[0]
    params_here = update.shape[1]
    block_width = min(512, params_here)
    blocks = params_here // block_width
    param_size = lax.axis_size("param")
    features_total = col_seeds.shape[0]

    def accumulate(block_index, summed):
        begin_at = block_index * block_width
        seed_rows = lax.dynamic_slice_in_dim(row_seeds, begin_at, block_width)
        columns = lax.dynamic_slice_in_dim(update, begin_at, block_width, 1)
        return summed + lax.dot_general(
            hashed_signs(seed_rows, col_seeds),
            columns,
            (((0,), (1,)), ((), ())),
            preferred_element_type=jnp.float32,
        )

    owned_rows = summed_on_arrival(
        lax.fori_loop(
            0,
            blocks,
            accumulate,
            jnp.zeros(
                (features_total // param_size * lax.axis_size("param"), examples_here), jnp.float32
            ),
        ),
        "param",
        0,
    )
    squares = of_everyone(jnp.sum(owned_rows * owned_rows, axis=0), "param")
    root_mean = jnp.sqrt(squares / features_total + 1e-06)
    features = (owned_rows / root_mean[None, :]).T
    labels = jnp.arange(GROUPS, dtype=jnp.int32)
    counts = jnp.sum((group_of[:, None] == labels[None, :]).astype(jnp.float32), axis=0)
    onehot = (group_of[:, None] == labels[None, :]).astype(jnp.float32)
    products = lax.dot_general(
        features,
        collect(features, "ex", 0),
        (((1,), (1,)), ((), ())),
        precision=lax.Precision.HIGHEST,
    )
    summed = jnp.dot(products, onehot, precision=lax.Precision.HIGHEST)
    totals = of_everyone(summed, "param")
    scores = totals / (counts[None, :] * features_total)
    return (features, scores)


def solution(mesh):
    in_specs = (P("ex", "param"), P("param"), P("param"), P("param"), P(), P())
    out_specs = (P("ex", "param"), P("ex", None))
    return jax.shard_map(shards, mesh=mesh, in_specs=in_specs, out_specs=out_specs, check_vma=False)
```

profile of v0, /device:TPU:1, one launch (start us, length us, event | category | flops | bytes accessed | tf_op | source)
XLA Modules:
  0.0 201.2 jit_solution(14881906123360369596)
XLA Ops:
  1.4 1.8 fusion.26
  3.1 68.7 %while.14 = (s32[]{:T(128)}, f32[8192,64]{0,1:T(8,128)S(1)}, s32[4096]{0:T(1024)}, s32[8192]{0:T(1024)}, bf16[64,4096]{1,0:T(8,128)(2,1)S(1)}, /*index=5*/s32[]{:T(128)}, s32[]{:T(128)}, s32[]{:T(128)}, s32[]{:T(128)}) while((s32[]{:T(128)}, f32[8192,64]{0,1:T(8,128)S(1)}, s32[4096]{0:T(1024)}, s32[8192]{0:T(1024)}, ...), condition=%wide.region_1.0_spmd.clone, body=%wide.region_0.0_spmd.clone.sunk | while | flops 584056832 | bytes 4298909 | solution.py:70
  3.2 0.8 dynamic_slice.21
  3.9 7.8 %convolution_add_fusion.2 = f32[8192,64]{0,1:T(8,128)S(1)} fusion(s32[8192]{0:T(1024)} %get-tuple-element.183, s32[512]{0:T(512)S(1)} %dynamic_slice.21, f32[8192,64]{0,1:T(8,128)S(1)} %get-tuple-element.172, pred[]{:T(512)S(6)} %compare.3, bf16[64,4096]{1,0:T(8,128)(2,1)S(1)} %get-tuple-element.184, s32[]{:T(128)S(6)} %select_n.10), kind=kOutput, calls=%fused_computation.8.clone.1 | convolution fusion | flops 584056832 | bytes 4294661 | tf_op jit(solution)/shard_map/while/body/eval_jaxpr/dot_general | solution.py:62
  11.7 0.8 dynamic_slice.21
  12.5 7.8 %convolution_add_fusion.2 = f32[8192,64]{0,1:T(8,128)S(1)} fusion(s32[8192]{0:T(1024)} %get-tuple-element.183, s32[512]{0:T(512)S(1)} %dynamic_slice.21, f32[8192,64]{0,1:T(8,128)S(1)} %get-tuple-element.172, pred[]{:T(512)S(6)} %compare.3, bf16[64,4096]{1,0:T(8,128)(2,1)S(1)} %get-tuple-element.184, s32[]{:T(128)S(6)} %select_n.10), kind=kOutput, calls=%fused_computation.8.clone.1 | convolution fusion | flops 584056832 | bytes 4294661 | tf_op jit(solution)/shard_map/while/body/eval_jaxpr/dot_general | solution.py:62
  20.3 0.8 dynamic_slice.21
  21.1 7.8 %convolution_add_fusion.2 = f32[8192,64]{0,1:T(8,128)S(1)} fusion(s32[8192]{0:T(1024)} %get-tuple-element.183, s32[512]{0:T(512)S(1)} %dynamic_slice.21, f32[8192,64]{0,1:T(8,128)S(1)} %get-tuple-element.172, pred[]{:T(512)S(6)} %compare.3, bf16[64,4096]{1,0:T(8,128)(2,1)S(1)} %get-tuple-element.184, s32[]{:T(128)S(6)} %select_n.10), kind=kOutput, calls=%fused_computation.8.clone.1 | convolution fusion | flops 584056832 | bytes 4294661 | tf_op jit(solution)/shard_map/while/body/eval_jaxpr/dot_general | solution.py:62
  28.9 0.8 dynamic_slice.21
  29.7 7.8 %convolution_add_fusion.2 = f32[8192,64]{0,1:T(8,128)S(1)} fusion(s32[8192]{0:T(1024)} %get-tuple-element.183, s32[512]{0:T(512)S(1)} %dynamic_slice.21, f32[8192,64]{0,1:T(8,128)S(1)} %get-tuple-element.172, pred[]{:T(512)S(6)} %compare.3, bf16[64,4096]{1,0:T(8,128)(2,1)S(1)} %get-tuple-element.184, s32[]{:T(128)S(6)} %select_n.10), kind=kOutput, calls=%fused_computation.8.clone.1 | convolution fusion | flops 584056832 | bytes 4294661 | tf_op jit(solution)/shard_map/while/body/eval_jaxpr/dot_general | solution.py:62
  37.5 0.8 dynamic_slice.21
  38.3 7.8 %convolution_add_fusion.2 = f32[8192,64]{0,1:T(8,128)S(1)} fusion(s32[8192]{0:T(1024)} %get-tuple-element.183, s32[512]{0:T(512)S(1)} %dynamic_slice.21, f32[8192,64]{0,1:T(8,128)S(1)} %get-tuple-element.172, pred[]{:T(512)S(6)} %compare.3, bf16[64,4096]{1,0:T(8,128)(2,1)S(1)} %get-tuple-element.184, s32[]{:T(128)S(6)} %select_n.10), kind=kOutput, calls=%fused_computation.8.clone.1 | convolution fusion | flops 584056832 | bytes 4294661 | tf_op jit(solution)/shard_map/while/body/eval_jaxpr/dot_general | solution.py:62
  46.1 0.8 dynamic_slice.21
  46.9 7.8 %convolution_add_fusion.2 = f32[8192,64]{0,1:T(8,128)S(1)} fusion(s32[8192]{0:T(1024)} %get-tuple-element.183, s32[512]{0:T(512)S(1)} %dynamic_slice.21, f32[8192,64]{0,1:T(8,128)S(1)} %get-tuple-element.172, pred[]{:T(512)S(6)} %compare.3, bf16[64,4096]{1,0:T(8,128)(2,1)S(1)} %get-tuple-element.184, s32[]{:T(128)S(6)} %select_n.10), kind=kOutput, calls=%fused_computation.8.clone.1 | convolution fusion | flops 584056832 | bytes 4294661 | tf_op jit(solution)/shard_map/while/body/eval_jaxpr/dot_general | solution.py:62
  55.5 7.8 %convolution_add_fusion.2 = f32[8192,64]{0,1:T(8,128)S(1)} fusion(s32[8192]{0:T(1024)} %get-tuple-element.183, s32[512]{0:T(512)S(1)} %dynamic_slice.21, f32[8192,64]{0,1:T(8,128)S(1)} %get-tuple-element.172, pred[]{:T(512)S(6)} %compare.3, bf16[64,4096]{1,0:T(8,128)(2,1)S(1)} %get-tuple-element.184, s32[]{:T(128)S(6)} %select_n.10), kind=kOutput, calls=%fused_computation.8.clone.1 | convolution fusion | flops 584056832 | bytes 4294661 | tf_op jit(solution)/shard_map/while/body/eval_jaxpr/dot_general | solution.py:62
  63.3 0.8 dynamic_slice.21
  64.0 7.8 %convolution_add_fusion.2 = f32[8192,64]{0,1:T(8,128)S(1)} fusion(s32[8192]{0:T(1024)} %get-tuple-element.183, s32[512]{0:T(512)S(1)} %dynamic_slice.21, f32[8192,64]{0,1:T(8,128)S(1)} %get-tuple-element.172, pred[]{:T(512)S(6)} %compare.3, bf16[64,4096]{1,0:T(8,128)(2,1)S(1)} %get-tuple-element.184, s32[]{:T(128)S(6)} %select_n.10), kind=kOutput, calls=%fused_computation.8.clone.1 | convolution fusion | flops 584056832 | bytes 4294661 | tf_op jit(solution)/shard_map/while/body/eval_jaxpr/dot_general | solution.py:62
  72.1 64.0 %all_to_all.21 = f32[64,128,64]{1,2,0:T(8,128)S(1)} all-to-all(f32[64,128,64]{1,2,0:T(8,128)S(1)} %copy_bitcast_fusion), channel_id=1, replica_groups=mesh['param'=64,'ex'=4] {'param'}, dimensions={0} | all-to-all | bytes 4194304 | tf_op jit(solution)/shard_map/all_to_all | solution.py:16
  136.4 14.9 %all_to_all.22 = f32[64,1,64]{2,1,0:T(1,128)S(1)} all-to-all(f32[64,1,64]{2,1,0:T(1,128)S(1)} %broadcast_in_dim.15), channel_id=1, replica_groups=mesh['param'=64,'ex'=4] {'param'}, dimensions={0} | all-to-all | bytes 32768 | tf_op jit(solution)/shard_map/all_to_all | solution.py:22
  151.5 8.8 %all_to_all.23 = f32[4,64,128]{2,1,0:T(8,128)S(1)} all-to-all(f32[4,64,128]{2,1,0:T(8,128)S(1)} %broadcast_in_dim.28), channel_id=1, replica_groups=mesh['param'=64,'ex'=4] {'ex'}, dimensions={0} | all-to-all | bytes 262144 | tf_op jit(solution)/shard_map/all_to_all | solution.py:22
  161.1 2.2 %reshape.32 = f32[64,1,3648]{2,1,0:T(1,128)} reshape(f32[64,57,64]{2,1,0:T(8,128)S(1)} %broadcast_bitcast_fusion) | data formatting | bytes 1867776
  163.2 6.4 %all-to-all-start.3 = ((f32[64,1,3648]{2,1,0:T(1,128)}), f32[64,1,3648]{2,1,0:T(1,128)S(1)}, u32[]{:S(2)}, u32[]{:S(2)}) async-start(f32[64,1,3648]{2,1,0:T(1,128)} %reshape.32), calls=%async_computation.3 | async-start | bytes 1900544 | tf_op jit(solution)/shard_map/all_to_all | solution.py:22
  169.7 26.3 %all-to-all-done.3 = f32[64,1,3648]{2,1,0:T(1,128)S(1)} async-done(((f32[64,1,3648]{2,1,0:T(1,128)}), f32[64,1,3648]{2,1,0:T(1,128)S(1)}, u32[]{:S(2)}, u32[]{:S(2)}) %all-to-all-start.3) | async-done | bytes 933920 | tf_op jit(solution)/shard_map/all_to_all | solution.py:22
  196.6 2.9 %reduce.1 = f32[64,3648]{1,0:T(8,128)S(1)} reduce(f32[64,1,3648]{2,1,0:T(1,128)S(1)} %all-to-all-done.3, f32[]{:T(128)} %broadcast.102), dimensions={1}, to_apply=%all_to_all.16.reduce_sub_computation | reduce | bytes 1867780 | tf_op jit(solution)/shard_map/all_to_all | solution.py:22
  (25 shorter events, 5.2 us)
Async XLA Ops:
  136.2 24.5 %copy-start.1 = (s32[256]{0:T(256)S(1)}, s32[256]{0:T(256)}, u32[]{:S(2)}) copy-start(s32[256]{0:T(256)} %param.13) | copy-start | bytes 3076
  151.5 11.7 %copy-start = (f32[64,128]{1,0:T(8,128)}, f32[64,128]{1,0:T(8,128)S(1)}, u32[]{:S(2)}) copy-start(f32[64,128]{1,0:T(8,128)S(1)} %fusion.30) | copy-start | bytes 98308
  163.2 32.8 %all-to-all-start.3 = ((f32[64,1,3648]{2,1,0:T(1,128)}), f32[64,1,3648]{2,1,0:T(1,128)S(1)}, u32[]{:S(2)}, u32[]{:S(2)}) async-start(f32[64,1,3648]{2,1,0:T(1,128)} %reshape.32), calls=%async_computation.3 | async-start | bytes 1900544 | tf_op jit(solution)/shard_map/all_to_all | solution.py:22
where the time goes:
time: 202 us; the launch traced here: 201 us
  blocking collectives  87.7 us (43%)
  matrix products  62.8 us (31%)
  waiting for transfers between devices  26.3 us (13%)
  local copies, waits for them, and re-layouts  10.8 us (5%)
  starting transfers between devices  6.36 us (3%)
  other arithmetic  6.14 us (3%)
    all_to_all x1, blocking collectives, summed_on_arrival(): lax.all_to_all(in_blocks(value, dim, count), axis, 0, 0, tiled=True)  64 us
    dot_general x8, matrix products, accumulate(): lax.dot_general(hashed_signs(seed_rows, col_seeds), columns, (((0,), (1,)...  62.4 us
    all_to_all x1, waiting for transfers between devices, from_everyone(): return lax.all_to_all(copies, axis, split_axis=0, concat_axis=0, tiled=True)  26.3 us
    all_to_all x2, blocking collectives, from_everyone(): return lax.all_to_all(copies, axis, split_axis=0, concat_axis=0, tiled=True)  23.7 us
    all_to_all x1, starting transfers between devices, from_everyone(): return lax.all_to_all(copies, axis, split_axis=0, concat_axis=0, tiled=True)  6.36 us
    dynamic_slice x8, local copies, waits for them, and re-layouts, accumulate(): seed_rows = lax.dynamic_slice_in_dim(row_seeds, begin_at, block_width)  6.11 us
  transfers between devices with their start and end apart: 1, of which 1 were waited for; matrix products, arithmetic and copies ran while one was open for 0% of the time, Pallas kernels for 0%

commit v1 on v0

v1 whole, which is shorter than its diff:
```python
import functools

import jax
import jax.numpy as jnp
from jax import lax
from jax.experimental import pallas as pl
from jax.experimental.pallas import tpu as pltpu
from jax.sharding import PartitionSpec as P

GROUPS = 57
X, Z, C, Y = 4, 8, 2, 4
XC = X * C
LANES = 128
ALONE = 8
MESH = pl.DeviceIdType.MESH
HIGH = lax.Precision.HIGHEST
F32 = jnp.float32

FACTOR = (739982445 << 4) & 0xFFFFFFFF
FACTOR = FACTOR - (1 << 32) if FACTOR >= 1 << 31 else FACTOR


def signs_of(product):
    mixed = product ^ (product >> 15)
    mixed = mixed * jnp.int32(FACTOR)
    mixed = mixed ^ (mixed >> 13)
    return jnp.where(mixed.astype(jnp.int16) < jnp.int16(0), jnp.bfloat16(-1), jnp.bfloat16(1))


def update_of(grad, mean, square):
    first = 0.9 * mean + 0.1 * grad
    second = 0.999 * square + 0.001 * grad * grad
    return (first / (jnp.sqrt(second) + 1e-08)).astype(jnp.bfloat16)


def contract(a, b):
    return lax.dot_general(a, b, (((1,), (1,)), ((), ())), precision=HIGH, preferred_element_type=F32)


def kernel(
    g_ref, m_ref, v_ref, r_ref, k_ref, group_ref,
    f_ref, s_ref,
    u_own, seeds,
    part_a, chip_a, sum_a, cols_a, rows_a, got_a,
    ybuf, send1, recv1, send2, recv2, out1, out2,
    cs_a, cr_a, xs_a, xr_a, zs_a, zr_a,
    ys, yr, s1s, s1r, s2s, s2r, o1s, o1r, o2s, o2r,
):
    me, y = lax.axis_index("param"), lax.axis_index("ex")
    x, z, c = me // (Z * C), (me // C) % Z, me % C
    xc = x * C + c
    examples, params = g_ref.shape
    features = k_ref.shape[0] * LANES

    def at(x_to, z_to, c_to):
        return ((x_to * Z + z_to) * C + c_to, y)

    def at_xc(to):
        return at(to // C, z, to % C)

    def send(src, dst, send_sem, recv_sem, device):
        return pltpu.make_async_remote_copy(
            src_ref=src, dst_ref=dst, send_sem=send_sem, recv_sem=recv_sem,
            device_id=device, device_id_type=MESH,
        )

    barrier = pltpu.get_barrier_semaphore()

    def greet(device):
        pl.semaphore_signal(barrier, inc=1, device_id=device, device_id_type=MESH)

    for d in range(1, XC):
        greet(at_xc((xc + d) % XC))
    for d in range(1, Z):
        greet(at(x, (z + d) % Z, c))
    for d in range(1, Y):
        greet((me, (y + d) % Y))

    def prepare(i, carry):
        lanes = pl.ds(pl.multiple_of(i * LANES, LANES), LANES)
        u_own[:, lanes] = update_of(g_ref[:, lanes], m_ref[pl.ds(i, 1), :], v_ref[pl.ds(i, 1), :])
        seeds[lanes, :] = jnp.broadcast_to(r_ref[pl.ds(i, 1), :], (LANES, LANES)).T
        return carry

    lax.fori_loop(0, params // LANES, prepare, 0)
    pl.semaphore_wait(barrier, (XC - 1) + (Z - 1) + (Y - 1))

    def place(t):
        return (x + 1 + t % X) % X, (z + 1 + t // X) % Z

    def chunk(update, depth, base, t):
        x_to, z_to = place(t)
        row = (x_to * Z + z_to) * C
        left, right = k_ref[pl.ds(row, 1), :], k_ref[pl.ds(row + 1, 1), :]
        strips = []
        for p in range(0, depth, 16):
            seed = seeds[pl.ds(pl.multiple_of(base + p, 16), 16), :]
            strips.append(jnp.concatenate([signs_of(seed * left), signs_of(seed * right)], axis=1))
        return jnp.dot(update, jnp.concatenate(strips, axis=0), preferred_element_type=F32)

    def chip_copy(t):
        return send(part_a.at[t, 1 - c], chip_a.at[t], cs_a.at[t], cr_a.at[t], at(x, z, 1 - c))

    def x_copy(t):
        slot = t // X, t % X
        return send(sum_a.at[slot], cols_a.at[slot], xs_a.at[slot], xr_a.at[slot], at((x + 1 + t % X) % X, z, c))

    def z_copy(group):
        return send(rows_a.at[group], got_a.at[group], zs_a.at[group], zr_a.at[group], at(x, (z + 1 + group) % Z, c))

    def after_chip(t):
        chip_copy(t).wait_recv()
        sum_a[t // X, t % X] = part_a[t, c] + chip_a[t]

        @pl.when(t % X < X - 1)
        def _():
            x_copy(t).start()

    def after_x(group):
        for j in range(X - 1):
            x_copy(group * X + j).wait_recv()
        rows_a[group] = sum_a[group, X - 1] + cols_a[group, 0] + cols_a[group, 1] + cols_a[group, 2]

    def step(t, carry):
        part = chunk(u_own[...], params, 0, t)
        part_a[t, 0] = part[:, :LANES]
        part_a[t, 1] = part[:, LANES:]
        chip_copy(t).start()

        @pl.when(t >= 1)
        def _():
            after_chip(t - 1)

        @pl.when((t % X == 2) & (t > X))
        def _():
            after_x(t // X - 1)
            z_copy(t // X - 1).start()

        return carry

    lax.fori_loop(0, Z * X, step, 0)
    after_chip(Z * X - 1)
    after_x(Z - 1)
    total = rows_a[Z - 1]
    for group in range(Z - 1):
        z_copy(group).wait_recv()
        total = total + got_a[group]

    ybuf[y] = total

    def y_copy(d):
        return send(ybuf.at[y], ybuf.at[y], ys.at[d - 1], yr.at[d - 1], (me, (y + d) % Y))

    for d in range(1, Y):
        y_copy(d).start()
    for d in range(1, Y):
        y_copy(d).wait_recv()
    every = ybuf[...].reshape(Y * examples, LANES)

    products = contract(total, every)
    squares = contract(jnp.ones((8, LANES), F32), every * every)
    send1[...] = jnp.zeros_like(send1)
    for j in range(Z):
        send1[j, :, : Y * examples] = products[j * XC : (j + 1) * XC, :]
        for h in range(2):
            send1[j, h : h + 1, Y * examples :] = squares[:1, h * LANES : (h + 1) * LANES]

    def send1_copy(d):
        to = (z + d) % Z
        return send(send1.at[to], recv1.at[d - 1], s1s.at[d - 1], s1r.at[d - 1], at(x, to, c))

    for d in range(1, Z):
        send1_copy(d).start()
    block = send1[z]
    for d in range(1, Z):
        send1_copy(d).wait_recv()
        block = block + recv1[d - 1]

    for j in range(XC):
        for h in range(2):
            send2[j, h : h + 1, :] = block[j : j + 1, h * LANES : (h + 1) * LANES]
            send2[j, 2 + h : 3 + h, :] = block[h : h + 1, Y * examples :]

    def send2_copy(d):
        to = (xc + d) % XC
        return send(send2.at[to], recv2.at[d - 1], s2s.at[d - 1], s2r.at[d - 1], at_xc(to))

    for d in range(1, XC):
        send2_copy(d).start()
    mine = send2[xc]
    for d in range(1, XC):
        send2_copy(d).wait_recv()
        mine = mine + recv2[d - 1]

    root_mean = jnp.sqrt(mine[2:4, :] / features + 1e-06)
    weights = mine[0:2, :] / root_mean
    example = y * examples + z * XC + xc
    places = LANES * lax.broadcasted_iota(jnp.int32, (2, LANES), 0) + lax.broadcasted_iota(jnp.int32, (2, LANES), 1)
    own_root = jnp.sum(jnp.where(places == example, root_mean, 0.0), keepdims=True)
    score, count = jnp.zeros((8, LANES), F32), jnp.zeros((8, LANES), F32)
    for h in range(2):
        labels = lax.broadcasted_iota(jnp.int32, (LANES, LANES), 0)
        onehot = (labels == group_ref[h : h + 1, :]).astype(F32)
        score = score + contract(jnp.broadcast_to(weights[h : h + 1, :], (8, LANES)), onehot)
        count = count + contract(jnp.ones((8, LANES), F32), onehot)
    count = jnp.where(count == 0, 1.0, count)
    out1[xc] = (score / own_root / (count * features))[:1, :]

    def out1_copy(d):
        return send(out1.at[xc], out1.at[xc], o1s.at[d - 1], o1r.at[d - 1], at_xc((xc + d) % XC))

    for d in range(1, XC):
        out1_copy(d).start()

    here = y * examples + lax.broadcasted_iota(jnp.int32, (examples, LANES), 0)
    lane = lax.broadcasted_iota(jnp.int32, (examples, LANES), 1)
    column = jnp.zeros((examples, 1), F32)
    for h in range(2):
        row = jnp.broadcast_to(root_mean[h : h + 1, :], (examples, LANES))
        column = column + jnp.sum(jnp.where(lane + h * LANES == here, row, 0.0), axis=1, keepdims=True)
    f_ref[...] = total / column

    for d in range(1, XC):
        out1_copy(d).wait_recv()
    out2[z] = out1[...]

    def out2_copy(d):
        return send(out1, out2.at[z], o2s.at[d - 1], o2r.at[d - 1], at(x, (z + d) % Z, c))

    for d in range(1, Z):
        out2_copy(d).start()
    for d in range(1, Z):
        out2_copy(d).wait_recv()
    for j in range(Z):
        for i in range(XC):
            s_ref[j * XC + i : j * XC + i + 1, :] = out2[j, i][:, :GROUPS]

    def chip_sent(t, carry):
        chip_copy(t).wait_send()

        @pl.when(t % X < X - 1)
        def _():
            x_copy(t).wait_send()

        return carry

    lax.fori_loop(0, Z * X, chip_sent, 0)
    for group in range(Z - 1):
        z_copy(group).wait_send()
    for d in range(1, Y):
        y_copy(d).wait_send()
    for d in range(1, Z):
        send1_copy(d).wait_send()
        out2_copy(d).wait_send()
    for d in range(1, XC):
        send2_copy(d).wait_send()
        out1_copy(d).wait_send()


def solution(mesh):
    def shards(gradients, m_state, v_state, row_seeds, col_seeds, group_of):
        examples, params = gradients.shape
        rows = (-1, LANES)
        dma, vmem = pltpu.SemaphoreType.DMA, pltpu.VMEM
        steps = Z * X
        block = (examples, LANES)
        wide = (Y * examples) + LANES
        return pl.pallas_call(
            kernel,
            out_shape=(
                jax.ShapeDtypeStruct((examples, LANES), F32),
                jax.ShapeDtypeStruct((examples, GROUPS), F32),
            ),
            in_specs=[pl.BlockSpec(memory_space=pltpu.VMEM)] * 6,
            out_specs=[pl.BlockSpec(memory_space=pltpu.VMEM)] * 2,
            scratch_shapes=[
                vmem((examples, params), jnp.bfloat16),
                vmem((params, LANES), jnp.int32),
                vmem((steps, 2, *block), F32),
                vmem((steps, *block), F32),
                vmem((Z, X, *block), F32),
                vmem((Z, X, *block), F32),
                vmem((Z, *block), F32),
                vmem((Z, *block), F32),
                vmem((Y, *block), F32),
                vmem((Z, XC, wide), F32),
                vmem((Z - 1, XC, wide), F32),
                vmem((XC, 4, LANES), F32),
                vmem((XC - 1, 4, LANES), F32),
                vmem((XC, 1, LANES), F32),
                vmem((Z, XC, 1, LANES), F32),
                dma((steps,)), dma((steps,)),
                dma((Z, X)), dma((Z, X)),
                dma((Z,)), dma((Z,)),
                dma((Y - 1,)), dma((Y - 1,)),
                dma((Z - 1,)), dma((Z - 1,)),
                dma((XC - 1,)), dma((XC - 1,)),
                dma((XC - 1,)), dma((XC - 1,)),
                dma((Z - 1,)), dma((Z - 1,)),
            ],
            compiler_params=pltpu.CompilerParams(
                collective_id=0, has_side_effects=True, vmem_limit_bytes=48 << 20
            ),
            name="features_and_scores",
        )(
            gradients, m_state.reshape(rows), v_state.reshape(rows), row_seeds.reshape(rows),
            col_seeds.reshape(rows), group_of.reshape(rows),
        )

    in_specs = (P("ex", "param"), P("param"), P("param"), P("param"), P(), P())
    out_specs = (P("ex", "param"), P("ex", None))
    return jax.shard_map(shards, mesh=mesh, in_specs=in_specs, out_specs=out_specs, check_vma=False)
```

time: 202 us -> 82.4 us (0.41)
  blocking collectives: 87.7 us -> 0 us
  Pallas kernels: 0 us -> 75.3 us
  matrix products: 62.8 us -> 0 us
  waiting for transfers between devices: 26.3 us -> 0 us
  starting transfers between devices: 6.36 us -> 0 us
  other arithmetic: 6.14 us -> 0 us
  local copies, waits for them, and re-layouts: 10.8 us -> 6.04 us
    all_to_all x3 -> x0, blocking collectives: 87.7 us -> none  [the longest x1 64 us: summed_on_arrival(): lax.all_to_all(in_blocks(value, dim, count), axis, 0, 0, tiled=True)]
    pallas_call x0 -> x1, Pallas kernels: none -> 75.3 us  [shards(): pl.pallas_call(kernel, out_shape=(jax.ShapeDtypeStruct((examples, LANES),...]
    dot_general x10 -> x0, matrix products: 62.8 us -> none  [the longest x8 62.4 us: accumulate(): lax.dot_general(hashed_signs(seed_rows, col_seeds), columns, (((0,), (1,)...]
    all_to_all x1 -> x0, waiting for transfers between devices: 26.3 us -> none  [from_everyone(): return lax.all_to_all(copies, axis, split_axis=0, concat_axis=0, tiled=True)]
    all_to_all x1 -> x0, starting transfers between devices: 6.36 us -> none  [from_everyone(): return lax.all_to_all(copies, axis, split_axis=0, concat_axis=0, tiled=True)]
    dynamic_slice x8 -> x0, local copies, waits for them, and re-layouts: 6.11 us -> none  [accumulate(): seed_rows = lax.dynamic_slice_in_dim(row_seeds, begin_at, block_width)]
    all_to_all x1 -> x0, other arithmetic: 2.9 us -> none  [from_everyone(): return lax.all_to_all(copies, axis, split_axis=0, concat_axis=0, tiled=True)]
    unnamed x8 -> x14, local copies, waits for them, and re-layouts: 3.85 us -> 6.04 us
  transfers between devices with their start and end apart: 1 -> 0, of which waited for: 1 -> 0; matrix products, arithmetic and copies ran while one was open for 0% -> 0% of each run, Pallas kernels for 0% -> 0%
where the time goes in v1:
time: 82.4 us; the launch traced here: 82 us
  Pallas kernels  75.3 us (91%)
  local copies, waits for them, and re-layouts  6.04 us (7%)
    pallas_call x1, Pallas kernels, shards(): pl.pallas_call(kernel, out_shape=(jax.ShapeDtypeStruct((examples, LANES),...  75.3 us
    unnamed x14, local copies, waits for them, and re-layouts  6.04 us

profile of v1, /device:TPU:1, one launch (start us, length us, event | category | flops | bytes accessed | tf_op | source)
XLA Modules:
  0.0 82.0 jit_solution(16847335784266354347)
XLA Ops:
  0.6 0.0 copy-start.5
  0.6 0.7 copy-done.5
  1.3 0.0 copy-start
  1.3 1.2 %copy-done = f32[64,4096]{1,0:T(8,128)S(1)} copy-done((f32[64,4096]{1,0:T(8,128)S(1)}, f32[64,4096]{1,0:T(8,128)}, u32[]{:S(2)}) %copy-start) | copy-done | bytes 1048600
  2.5 0.0 copy-start.1
  2.5 0.8 copy-done.1
  3.3 0.0 copy-start.2
  3.3 0.7 copy-done.2
  4.0 0.0 copy-start.3
  4.0 0.7 copy-done.3
  4.7 0.0 copy-start.4
  4.7 0.7 copy-done.4
  5.4 75.3 %features_and_scores.1 = (f32[64,128]{1,0:T(8,128)S(1)}, f32[64,57]{1,0:T(8,128)S(1)}) custom-call(f32[64,4096]{1,0:T(8,128)S(1)} %copy-done, f32[32,128]{1,0:T(8,128)S(1)} %bitcast.6, f32[32,128]{1,0:T(8,128)S(1)} %bitcast.7, s32[32,128]{1,0:T(8,128)S(1)} %bitcast.8, s32[64,128]{1,0:T(8,128)S(1)} %bitcast.5, s32[2,128]{1,0:T(2,128)S(1)} %bitcast.9), custom_call_target="tpu_custom_call" | custom-call | tf_op jit(solution)/shard_map/features_and_scores/pallas_call | solution.py:268
  80.8 0.6 copy.10
  81.4 0.6 copy.11
Async XLA Ops:
  0.6 0.7 copy-start.5
  1.3 1.2 %copy-start = (f32[64,4096]{1,0:T(8,128)S(1)}, f32[64,4096]{1,0:T(8,128)}, u32[]{:S(2)}) copy-start(f32[64,4096]{1,0:T(8,128)} %g_ref.1) | copy-start | bytes 3145732
  2.5 0.8 copy-start.1
  3.3 0.7 copy-start.2
  4.0 0.7 copy-start.3
  4.7 0.7 copy-start.4

commit v2 on v1

v2 whole, which is shorter than its diff:
```python
import functools

import jax
import jax.numpy as jnp
from jax import lax
from jax.experimental import pallas as pl
from jax.experimental.pallas import tpu as pltpu
from jax.sharding import PartitionSpec as P

GROUPS = 57
X, Z, C, Y = 4, 8, 2, 4
XC = X * C
LANES = 128
ALONE = 3
LATE = 3
LAST = Z * X - 1
FARTHEST_FIRST = (4, 3, 5, 2, 6, 1, 7)
MESH = pl.DeviceIdType.MESH
HIGH = lax.Precision.HIGHEST
F32 = jnp.float32

FACTOR = (739982445 << 4) & 0xFFFFFFFF
FACTOR = FACTOR - (1 << 32) if FACTOR >= 1 << 31 else FACTOR


def signs_of(product):
    mixed = product ^ (product >> 15)
    mixed = mixed * jnp.int32(FACTOR)
    mixed = mixed ^ (mixed >> 13)
    return jnp.where(mixed.astype(jnp.int16) < jnp.int16(0), jnp.bfloat16(-1), jnp.bfloat16(1))


def update_of(grad, mean, square):
    first = 0.9 * mean + 0.1 * grad
    second = 0.999 * square + 0.001 * grad * grad
    return (first / (jnp.sqrt(second) + 1e-08)).astype(jnp.bfloat16)


def contract(a, b):
    return lax.dot_general(a, b, (((1,), (1,)), ((), ())), precision=HIGH, preferred_element_type=F32)


def remote(src, dst, send_sem, recv_sem, device):
    return pltpu.make_async_remote_copy(
        src_ref=src, dst_ref=dst, send_sem=send_sem, recv_sem=recv_sem,
        device_id=device, device_id_type=MESH,
    )


class Sums:
    def __init__(self, begin, at, x, z, c, buffers, semaphores):
        self.begin, self.at, self.x, self.z, self.c = begin, at, x, z, c
        self.part, self.chip, self.sum, self.cols, self.rows, self.got = buffers
        self.cs, self.cr, self.xs, self.xr, self.zs, self.zr = semaphores

    def slot(self, t):
        return t // X - self.begin, t % X

    def put(self, t, value):
        i = t - self.begin * X
        self.part[i, 0] = value[:, :LANES]
        self.part[i, 1] = value[:, LANES:]

    def chip_copy(self, t):
        i = t - self.begin * X
        return remote(
            self.part.at[i, 1 - self.c], self.chip.at[i], self.cs.at[i], self.cr.at[i],
            self.at(self.x, self.z, 1 - self.c),
        )

    def x_copy(self, t):
        i = self.slot(t)
        to = self.at((self.x + 1 + t % X) % X, self.z, self.c)
        return remote(self.sum.at[i], self.cols.at[i], self.xs.at[i], self.xr.at[i], to)

    def z_copy(self, group):
        i = group - self.begin
        to = self.at(self.x, (self.z + 1 + group) % Z, self.c)
        return remote(self.rows.at[i], self.got.at[i], self.zs.at[i], self.zr.at[i], to)

    def after_chip(self, t):
        i = t - self.begin * X
        self.chip_copy(t).wait_recv()
        self.sum[self.slot(t)] = self.part[i, self.c] + self.chip[i]

        @pl.when(t % X < X - 1)
        def _():
            self.x_copy(t).start()

    def after_x(self, group):
        i = group - self.begin
        for j in range(X - 1):
            self.x_copy(group * X + j).wait_recv()
        self.rows[i] = self.sum[i, X - 1] + self.cols[i, 0] + self.cols[i, 1] + self.cols[i, 2]

    def sent(self, end):
        def one(t, carry):
            self.chip_copy(t).wait_send()

            @pl.when(t % X < X - 1)
            def _():
                self.x_copy(t).wait_send()

            return carry

        lax.fori_loop(self.begin * X, end * X, one, 0)
        for group in range(self.begin, min(end, Z - 1)):
            self.z_copy(group).wait_send()


def kernel(
    g_in, m_in, v_in, r_in, k_in, group_in,
    f_ref, s_ref,
    g_ref, m_ref, v_ref, r_ref, k_ref, group_ref, in_sems,
    u_own, u_both, g_other, seeds,
    part_a, chip_a, sum_a, cols_a, rows_a, got_a,
    part_b, chip_b, sum_b, cols_b, rows_b, got_b,
    ybuf, blocks, send1, recv1, planes, scored,
    gs, gr,
    cs_a, cr_a, xs_a, xr_a, zs_a, zr_a,
    cs_b, cr_b, xs_b, xr_b, zs_b, zr_b,
    ys, yr, s1s, s1r, s2s, s2r, o1s, o1r,
):
    me, y = lax.axis_index("param"), lax.axis_index("ex")
    x, z, c = me // (Z * C), (me // C) % Z, me % C
    xc = x * C + c
    side = y % 2
    partner = (me, y + 1 - 2 * side)
    examples, params = g_ref.shape
    half = params // 2
    features = k_ref.shape[0] * LANES
    send = remote

    inputs = [
        pltpu.make_async_copy(src, dst, in_sems.at[i])
        for i, (src, dst) in enumerate(
            [(g_in, g_ref), (m_in, m_ref), (v_in, v_ref), (r_in, r_ref), (k_in, k_ref), (group_in, group_ref)]
        )
    ]
    for copy in inputs:
        copy.start()

    def at(x_to, z_to, c_to):
        return ((x_to * Z + z_to) * C + c_to, y)

    def at_xc(to):
        return at(to // C, z, to % C)

    barrier = pltpu.get_barrier_semaphore()

    def greet(device):
        pl.semaphore_signal(barrier, inc=1, device_id=device, device_id_type=MESH)

    for d in FARTHEST_FIRST:
        greet(at(x, (z + d) % Z, c))
    for d in range(1, XC):
        greet(at_xc((xc + d) % XC))
    for d in range(1, Y):
        greet((me, (y + d) % Y))
    for copy in inputs:
        copy.wait()

    def prepare(i, carry):
        for k in range(4):
            row = i * 4 + k
            lanes = pl.ds(pl.multiple_of(row * LANES, LANES), LANES)
            u_own[:, lanes] = update_of(g_ref[:, lanes], m_ref[pl.ds(row, 1), :], v_ref[pl.ds(row, 1), :])
            seeds[lanes, :] = jnp.broadcast_to(r_ref[pl.ds(row, 1), :], (LANES, LANES)).T
        return carry

    lax.fori_loop(0, params // LANES // 4, prepare, 0)

    def chunk(update, depth, base, t):
        x_to, z_to = (x + 1 + t % X) % X, (z + 1 + t // X) % Z
        row = (x_to * Z + z_to) * C
        left, right = k_ref[pl.ds(row, 1), :], k_ref[pl.ds(row + 1, 1), :]
        strips = []
        for p in range(0, depth, 16):
            seed = seeds[pl.ds(pl.multiple_of(base + p, 16), 16), :]
            strips.append(jnp.concatenate([signs_of(seed * left), signs_of(seed * right)], axis=1))
        return jnp.dot(update, jnp.concatenate(strips, axis=0), preferred_element_type=F32)

    alone = Sums(
        0, at, x, z, c,
        (part_a, chip_a, sum_a, cols_a, rows_a, got_a), (cs_a, cr_a, xs_a, xr_a, zs_a, zr_a),
    )
    both = Sums(
        ALONE, at, x, z, c,
        (part_b, chip_b, sum_b, cols_b, rows_b, got_b), (cs_b, cr_b, xs_b, xr_b, zs_b, zr_b),
    )
    exchange = send(
        g_ref.at[:, pl.ds(pl.multiple_of((1 - side) * half, half), half)], g_other, gs.at[0], gr.at[0], partner
    )

    def early(t, carry):
        alone.put(t, chunk(u_own[...], params, 0, t))
        return carry

    def step_alone(t, carry):
        early(t, carry)
        alone.chip_copy(t).start()

        @pl.when(t == LATE + 1)
        def _():
            for i in range(LATE):
                alone.after_chip(i)

        alone.after_chip(t - 1)

        @pl.when((t % X == 2) & (t >= X + 2))
        def _():
            alone.after_x(t // X - 1)
            alone.z_copy(t // X - 1).start()

        return carry

    lax.fori_loop(0, LATE + 1, early, 0)
    pl.semaphore_wait(barrier, (XC - 1) + (Z - 1) + (Y - 1))
    exchange.start()
    for t in range(LATE + 1):
        alone.chip_copy(t).start()
    lax.fori_loop(LATE + 1, ALONE * X, step_alone, 0)

    u_both[side] = u_own[:, pl.ds(pl.multiple_of(side * half, half), half)]
    exchange.wait_recv()

    def prepare_other(i, carry):
        for k in range(4):
            lanes = pl.ds(pl.multiple_of((i * 4 + k) * LANES, LANES), LANES)
            row = side * (half // LANES) + i * 4 + k
            u_both[1 - side, :, lanes] = update_of(g_other[:, lanes], m_ref[pl.ds(row, 1), :], v_ref[pl.ds(row, 1), :])
        return carry

    lax.fori_loop(0, half // LANES // 4, prepare_other, 0)

    def step_both(t, carry):
        both.put(t, chunk(u_both[...].reshape(2 * examples, half), half, side * half, t))
        both.chip_copy(t).start()

        @pl.when(t == ALONE * X)
        def _():
            alone.after_chip(ALONE * X - 1)

        @pl.when(t == ALONE * X + 4)
        def _():
            alone.after_x(ALONE - 1)
            alone.z_copy(ALONE - 1).start()

        @pl.when(t >= ALONE * X + 2)
        def _():
            both.after_chip(t - 2)

        @pl.when((t % X == 2) & (t >= ALONE * X + 10))
        def _():
            both.after_x(t // X - 2)
            both.z_copy(t // X - 2).start()

        return carry

    lax.fori_loop(ALONE * X, Z * X, step_both, 0)
    both.after_chip(LAST - 1)
    both.after_x(Z - 2)
    both.z_copy(Z - 2).start()
    both.after_chip(LAST)
    own = jnp.zeros((examples, LANES), F32)
    for group in range(ALONE):
        alone.z_copy(group).wait_recv()
        own = own + got_a[group]
    both.after_x(Z - 1)
    pair = rows_b[Z - 1 - ALONE]
    for group in range(ALONE, Z - 1):
        both.z_copy(group).wait_recv()
        pair = pair + got_b[group - ALONE]

    ybuf[y] = pair.reshape(2, examples, LANES)
    ybuf[y, side] = ybuf[y, side] + own

    def y_copy(d):
        return send(ybuf.at[y], ybuf.at[y], ys.at[d - 1], yr.at[d - 1], (me, (y + d) % Y))

    for d in range(1, Y):
        y_copy(d).start()
    for d in range(1, Y):
        y_copy(d).wait_recv()
    for e in range(Y):
        blocks[e] = ybuf[e, e % 2] + ybuf[e + 1 - 2 * (e % 2), e % 2]
    total = blocks[y]
    every = blocks[...].reshape(Y * examples, LANES)

    products = contract(total, every)
    squares = contract(jnp.ones((8, LANES), F32), every * every)
    send1[...] = jnp.zeros_like(send1)
    for j in range(XC):
        send1[j, :, : Y * examples] = products[j * Z : (j + 1) * Z, :]
        for h in range(2):
            send1[j, h : h + 1, Y * examples :] = squares[:1, h * LANES : (h + 1) * LANES]

    def send1_copy(d):
        to = (xc + d) % XC
        return send(send1.at[to], recv1.at[d - 1], s1s.at[d - 1], s1r.at[d - 1], at_xc(to))

    for d in range(1, XC):
        send1_copy(d).start()
    block = send1[xc]
    for d in range(1, XC):
        send1_copy(d).wait_recv()
        block = block + recv1[d - 1]
    planes[z] = block

    def plane_copy(d):
        return send(planes.at[z], planes.at[z], s2s.at[d - 1], s2r.at[d - 1], at(x, (z + d) % Z, c))

    for d in FARTHEST_FIRST:
        plane_copy(d).start()
    for d in range(1, Z):
        plane_copy(d).wait_recv()
    block = planes[0]
    for j in range(1, Z):
        block = block + planes[j]

    root_mean = jnp.sqrt(block[:2, Y * examples :] / features + 1e-06)
    example = y * examples + xc * Z + lax.broadcasted_iota(jnp.int32, (Z, LANES), 0)
    lane = lax.broadcasted_iota(jnp.int32, (Z, LANES), 1)
    labels = lax.broadcasted_iota(jnp.int32, (LANES, LANES), 0)
    own_root = jnp.zeros((Z, 1), F32)
    score, count = jnp.zeros((Z, LANES), F32), jnp.zeros((Z, LANES), F32)
    for h in range(2):
        row = jnp.broadcast_to(root_mean[h : h + 1, :], (Z, LANES))
        own_root = own_root + jnp.sum(jnp.where(lane + h * LANES == example, row, 0.0), axis=1, keepdims=True)
        onehot = (labels == group_ref[h : h + 1, :]).astype(F32)
        score = score + contract(block[:, h * LANES : (h + 1) * LANES] / row, onehot)
        count = count + contract(jnp.ones((Z, LANES), F32), onehot)
    count = jnp.where(count == 0, 1.0, count)
    scored[xc] = score / own_root / (count * features)

    def score_copy(d):
        return send(scored.at[xc], scored.at[xc], o1s.at[d - 1], o1r.at[d - 1], at_xc((xc + d) % XC))

    for d in range(1, XC):
        score_copy(d).start()

    here = y * examples + lax.broadcasted_iota(jnp.int32, (examples, LANES), 0)
    lane = lax.broadcasted_iota(jnp.int32, (examples, LANES), 1)
    column = jnp.zeros((examples, 1), F32)
    for h in range(2):
        row = jnp.broadcast_to(root_mean[h : h + 1, :], (examples, LANES))
        column = column + jnp.sum(jnp.where(lane + h * LANES == here, row, 0.0), axis=1, keepdims=True)
    f_ref[...] = total / column

    for d in range(1, XC):
        score_copy(d).wait_recv()
    s_ref[...] = scored[...].reshape(examples, LANES)[:, :GROUPS]

    exchange.wait_send()
    alone.sent(ALONE)
    both.sent(Z)
    for d in range(1, Y):
        y_copy(d).wait_send()
    for d in range(1, XC):
        send1_copy(d).wait_send()
        score_copy(d).wait_send()
    for d in range(1, Z):
        plane_copy(d).wait_send()


def solution(mesh):
    def shards(gradients, m_state, v_state, row_seeds, col_seeds, group_of):
        examples, params = gradients.shape
        rows = (-1, LANES)
        dma, vmem = pltpu.SemaphoreType.DMA, pltpu.VMEM
        wide = (Y * examples) + LANES

        def buffers(groups, rows):
            block = (rows, LANES)
            return [
                vmem((groups * X, 2, *block), F32),
                vmem((groups * X, *block), F32),
                vmem((groups, X, *block), F32),
                vmem((groups, X, *block), F32),
                vmem((groups, *block), F32),
                vmem((groups, *block), F32),
            ]

        def semaphores(groups):
            return [
                dma((groups * X,)), dma((groups * X,)),
                dma((groups, X)), dma((groups, X)),
                dma((groups,)), dma((groups,)),
            ]

        arguments = [
            gradients, m_state.reshape(rows), v_state.reshape(rows), row_seeds.reshape(rows),
            col_seeds.reshape(rows), group_of.reshape(rows),
        ]
        return pl.pallas_call(
            kernel,
            out_shape=(
                jax.ShapeDtypeStruct((examples, LANES), F32),
                jax.ShapeDtypeStruct((examples, GROUPS), F32),
            ),
            in_specs=[pl.BlockSpec(memory_space=pltpu.HBM)] * 6,
            out_specs=[pl.BlockSpec(memory_space=pltpu.VMEM)] * 2,
            scratch_shapes=[
                *[vmem(array.shape, array.dtype) for array in arguments],
                dma((6,)),
                vmem((examples, params), jnp.bfloat16),
                vmem((2, examples, params // 2), jnp.bfloat16),
                vmem((examples, params // 2), F32),
                vmem((params, LANES), jnp.int32),
                *buffers(ALONE, examples),
                *buffers(Z - ALONE, 2 * examples),
                vmem((Y, 2, examples, LANES), F32),
                vmem((Y, examples, LANES), F32),
                vmem((XC, Z, wide), F32),
                vmem((XC - 1, Z, wide), F32),
                vmem((Z, Z, wide), F32),
                vmem((XC, Z, LANES), F32),
                dma((1,)), dma((1,)),
                *semaphores(ALONE),
                *semaphores(Z - ALONE),
                dma((Y - 1,)), dma((Y - 1,)),
                dma((XC - 1,)), dma((XC - 1,)),
                dma((Z - 1,)), dma((Z - 1,)),
                dma((XC - 1,)), dma((XC - 1,)),
            ],
            compiler_params=pltpu.CompilerParams(
                collective_id=0, has_side_effects=True, vmem_limit_bytes=63 << 20
            ),
            name="features_and_scores",
        )(*arguments)

    in_specs = (P("ex", "param"), P("param"), P("param"), P("param"), P(), P())
    out_specs = (P("ex", "param"), P("ex", None))
    return jax.shard_map(shards, mesh=mesh, in_specs=in_specs, out_specs=out_specs, check_vma=False)
```

time: 82.4 us -> 74.3 us (0.902)
  local copies, waits for them, and re-layouts: 6.04 us -> 2 us
  Pallas kernels: 75.3 us -> 71.5 us
    unnamed x14 -> x4, local copies, waits for them, and re-layouts: 6.04 us -> 2 us
    pallas_call x1, Pallas kernels: 75.3 us -> 71.5 us  [shards(): pl.pallas_call(kernel, out_shape=(jax.ShapeDtypeStruct((examples, LANES),...]
where the time goes in v2:
time: 74.3 us; the launch traced here: 74.1 us
  Pallas kernels  71.5 us (96%)
  local copies, waits for them, and re-layouts  2 us (3%)
    pallas_call x1, Pallas kernels, shards(): pl.pallas_call(kernel, out_shape=(jax.ShapeDtypeStruct((examples, LANES),...  71.5 us
    unnamed x4, local copies, waits for them, and re-layouts  2 us

profile of v2, /device:TPU:1, one launch (start us, length us, event | category | flops | bytes accessed | tf_op | source)
XLA Modules:
  0.0 74.1 jit_solution(8608709337027039966)
XLA Ops:
  0.6 71.5 %features_and_scores.1 = (f32[64,128]{1,0:T(8,128)}, f32[64,57]{1,0:T(8,128)}) custom-call(f32[64,4096]{1,0:T(8,128)} %g_in.1, f32[32,128]{1,0:T(8,128)} %bitcast.6, f32[32,128]{1,0:T(8,128)} %bitcast.7, s32[32,128]{1,0:T(8,128)} %bitcast.8, s32[64,128]{1,0:T(8,128)} %bitcast.5, s32[2,128]{1,0:T(2,128)} %bitcast.9), custom_call_target="tpu_custom_call" | custom-call | tf_op jit(solution)/shard_map/features_and_scores/pallas_call | solution.py:395
  72.1 0.0 copy-start
  72.1 1.4 %copy.10 = f32[64,128]{1,0:T(8,128)} copy(f32[64,128]{1,0:T(8,128)} %get-tuple-element.4) | data formatting | bytes 65536
  73.5 0.0 copy-done
  73.5 0.6 copy.11
Async XLA Ops:
  72.1 1.4 %copy-start = (f32[64,57]{1,0:T(8,128)S(1)}, f32[64,57]{1,0:T(8,128)}, u32[]{:S(2)}) copy-start(f32[64,57]{1,0:T(8,128)} %get-tuple-element.5) | copy-start | bytes 43780

commit v3 on v2

--- a/solution.py
+++ b/solution.py
@@ -11,8 +11,8 @@
 X, Z, C, Y = 4, 8, 2, 4
 XC = X * C
 LANES = 128
-ALONE = 3
-LATE = 3
+ALONE = 4
+LATE = 2
 LAST = Z * X - 1
 FARTHEST_FIRST = (4, 3, 5, 2, 6, 1, 7)
 MESH = pl.DeviceIdType.MESH
@@ -192,34 +192,41 @@
         g_ref.at[:, pl.ds(pl.multiple_of((1 - side) * half, half), half)], g_other, gs.at[0], gr.at[0], partner
     )
 
-    def early(t, carry):
+    def pair_alone(i, carry):
+        t = 2 * i
         alone.put(t, chunk(u_own[...], params, 0, t))
+        alone.put(t + 1, chunk(u_own[...], params, 0, t + 1))
+
+        @pl.when(t == LATE)
+        def _():
+            pl.semaphore_wait(barrier, (XC - 1) + (Z - 1) + (Y - 1))
+            exchange.start()
+            for early in range(LATE):
+                alone.chip_copy(early).start()
+
+        @pl.when(t >= LATE)
+        def _():
+            alone.chip_copy(t).start()
+            alone.chip_copy(t + 1).start()
+
+        @pl.when(t == LATE + 2)
+        def _():
+            for early in range(LATE):
+                alone.after_chip(early)
+
+        @pl.when(t >= LATE + 2)
+        def _():
+            alone.after_chip(t - 2)
+            alone.after_chip(t - 1)
+
+        @pl.when((t % X == 0) & (t >= LATE + 6))
+        def _():
+            alone.after_x(t // X - 2)
+            alone.z_copy(t // X - 2).start()
+
         return carry
 
-    def step_alone(t, carry):
-        early(t, carry)
-        alone.chip_copy(t).start()
-
-        @pl.when(t == LATE + 1)
-        def _():
-            for i in range(LATE):
-                alone.after_chip(i)
-
-        alone.after_chip(t - 1)
-
-        @pl.when((t % X == 2) & (t >= X + 2))
-        def _():
-            alone.after_x(t // X - 1)
-            alone.z_copy(t // X - 1).start()
-
-        return carry
-
-    lax.fori_loop(0, LATE + 1, early, 0)
-    pl.semaphore_wait(barrier, (XC - 1) + (Z - 1) + (Y - 1))
-    exchange.start()
-    for t in range(LATE + 1):
-        alone.chip_copy(t).start()
-    lax.fori_loop(LATE + 1, ALONE * X, step_alone, 0)
+    lax.fori_loop(0, ALONE * X // 2, pair_alone, 0)
 
     u_both[side] = u_own[:, pl.ds(pl.multiple_of(side * half, half), half)]
     exchange.wait_recv()
@@ -233,31 +240,55 @@
 
     lax.fori_loop(0, half // LANES // 4, prepare_other, 0)
 
-    def step_both(t, carry):
+    def chunk_both(t):
         both.put(t, chunk(u_both[...].reshape(2 * examples, half), half, side * half, t))
+
+    def pair_both(i, carry):
+        t = ALONE * X + 2 * i
+        chunk_both(t)
+        chunk_both(t + 1)
         both.chip_copy(t).start()
-
-        @pl.when(t == ALONE * X)
-        def _():
+        both.chip_copy(t + 1).start()
+
+        @pl.when(i == 0)
+        def _():
+            alone.after_chip(ALONE * X - 2)
             alone.after_chip(ALONE * X - 1)
-
-        @pl.when(t == ALONE * X + 4)
+            alone.after_x(ALONE - 2)
+            alone.z_copy(ALONE - 2).start()
+
+        @pl.when(i == 3)
         def _():
             alone.after_x(ALONE - 1)
             alone.z_copy(ALONE - 1).start()
 
-        @pl.when(t >= ALONE * X + 2)
+        @pl.when(i >= 1)
         def _():
             both.after_chip(t - 2)
-
-        @pl.when((t % X == 2) & (t >= ALONE * X + 10))
-        def _():
-            both.after_x(t // X - 2)
-            both.z_copy(t // X - 2).start()
+            both.after_chip(t - 1)
+
+        @pl.when((i % 2 == 1) & (i >= 5))
+        def _():
+            group = ALONE + (i - 5) // 2
+            both.after_x(group)
+            both.z_copy(group).start()
 
         return carry
 
-    lax.fori_loop(ALONE * X, Z * X, step_both, 0)
+    def step_both(t, carry):
+        chunk_both(t)
+        both.chip_copy(t).start()
+        both.after_chip(t - 2)
+
+        @pl.when(t == LAST - 1)
+        def _():
+            both.after_x(Z - 3)
+            both.z_copy(Z - 3).start()
+
+        return carry
+
+    lax.fori_loop(0, (Z - 1 - ALONE) * X // 2, pair_both, 0)
+    lax.fori_loop((Z - 1) * X, Z * X, step_both, 0)
     both.after_chip(LAST - 1)
     both.after_x(Z - 2)
     both.z_copy(Z - 2).start()
@@ -280,6 +311,9 @@
 
     for d in range(1, Y):
         y_copy(d).start()
+    exchange.wait_send()
+    alone.sent(ALONE)
+    both.sent(Z)
     for d in range(1, Y):
         y_copy(d).wait_recv()
     for e in range(Y):
@@ -301,6 +335,8 @@
 
     for d in range(1, XC):
         send1_copy(d).start()
+    for d in range(1, Y):
+        y_copy(d).wait_send()
     block = send1[xc]
     for d in range(1, XC):
         send1_copy(d).wait_recv()
@@ -312,6 +348,8 @@
 
     for d in FARTHEST_FIRST:
         plane_copy(d).start()
+    for d in range(1, XC):
+        send1_copy(d).wait_send()
     for d in range(1, Z):
         plane_copy(d).wait_recv()
     block = planes[0]
@@ -338,6 +376,8 @@
 
     for d in range(1, XC):
         score_copy(d).start()
+    for d in range(1, Z):
+        plane_copy(d).wait_send()
 
     here = y * examples + lax.broadcasted_iota(jnp.int32, (examples, LANES), 0)
     lane = lax.broadcasted_iota(jnp.int32, (examples, LANES), 1)
@@ -351,16 +391,8 @@
         score_copy(d).wait_recv()
     s_ref[...] = scored[...].reshape(examples, LANES)[:, :GROUPS]
 
-    exchange.wait_send()
-    alone.sent(ALONE)
-    both.sent(Z)
-    for d in range(1, Y):
-        y_copy(d).wait_send()
-    for d in range(1, XC):
-        send1_copy(d).wait_send()
+    for d in range(1, XC):
         score_copy(d).wait_send()
-    for d in range(1, Z):
-        plane_copy(d).wait_send()
 
 
 def solution(mesh):
@@ -424,10 +456,10 @@
                 dma((XC - 1,)), dma((XC - 1,)),
             ],
             compiler_params=pltpu.CompilerParams(
-                collective_id=0, has_side_effects=True, vmem_limit_bytes=63 << 20
+                collective_id=0, has_side_effects=True, vmem_limit_bytes=48 << 20
             ),
             name="features_and_scores",
-        )(*arguments)
+        )(*[pltpu.with_memory_space_constraint(array, pltpu.HBM) for array in arguments])
 
     in_specs = (P("ex", "param"), P("param"), P("param"), P("param"), P(), P())
     out_specs = (P("ex", "param"), P("ex", None))

time: 74.3 us -> 69.5 us (0.935)
  Pallas kernels: 71.5 us -> 67.5 us
  local copies, waits for them, and re-layouts: 2 us -> 1.23 us
    pallas_call x1, Pallas kernels: 71.5 us -> 67.5 us  [shards(): pl.pallas_call(kernel, out_shape=(jax.ShapeDtypeStruct((examples, LANES),...]
    unnamed x4 -> x2, local copies, waits for them, and re-layouts: 2 us -> 1.23 us
where the time goes in v3:
time: 69.5 us; the launch traced here: 69.4 us
  Pallas kernels  67.5 us (97%)
  local copies, waits for them, and re-layouts  1.23 us (2%)
    pallas_call x1, Pallas kernels, shards(): pl.pallas_call(kernel, out_shape=(jax.ShapeDtypeStruct((examples, LANES),...  67.5 us

profile of v3, /device:TPU:1, one launch (start us, length us, event | category | flops | bytes accessed | tf_op | source)
XLA Modules:
  0.0 69.4 jit_solution(2766414185171978212)
XLA Ops:
  0.6 67.5 %features_and_scores.1 = (f32[64,128]{1,0:T(8,128)S(1)}, f32[64,57]{1,0:T(8,128)S(1)}) custom-call(f32[64,4096]{1,0:T(8,128)} %g_in.1, f32[32,128]{1,0:T(8,128)} %bitcast.6, f32[32,128]{1,0:T(8,128)} %bitcast.7, s32[32,128]{1,0:T(8,128)} %bitcast.8, s32[64,128]{1,0:T(8,128)} %bitcast.5, s32[2,128]{1,0:T(2,128)} %bitcast.9), custom_call_target="tpu_custom_call" | custom-call | tf_op jit(solution)/shard_map/features_and_scores/pallas_call | solution.py:427
  68.2 0.6 copy.10
  68.8 0.6 copy.11

commit v4 on v3

--- a/solution.py
+++ b/solution.py
@@ -12,7 +12,6 @@
 XC = X * C
 LANES = 128
 ALONE = 4
-LATE = 2
 LAST = Z * X - 1
 FARTHEST_FIRST = (4, 3, 5, 2, 6, 1, 7)
 MESH = pl.DeviceIdType.MESH
@@ -197,29 +196,20 @@
         alone.put(t, chunk(u_own[...], params, 0, t))
         alone.put(t + 1, chunk(u_own[...], params, 0, t + 1))
 
-        @pl.when(t == LATE)
+        @pl.when(i == 0)
         def _():
             pl.semaphore_wait(barrier, (XC - 1) + (Z - 1) + (Y - 1))
             exchange.start()
-            for early in range(LATE):
-                alone.chip_copy(early).start()
-
-        @pl.when(t >= LATE)
-        def _():
-            alone.chip_copy(t).start()
-            alone.chip_copy(t + 1).start()
-
-        @pl.when(t == LATE + 2)
-        def _():
-            for early in range(LATE):
-                alone.after_chip(early)
-
-        @pl.when(t >= LATE + 2)
+
+        alone.chip_copy(t).start()
+        alone.chip_copy(t + 1).start()
+
+        @pl.when(i >= 1)
         def _():
             alone.after_chip(t - 2)
             alone.after_chip(t - 1)
 
-        @pl.when((t % X == 0) & (t >= LATE + 6))
+        @pl.when((t % X == 0) & (t >= 2 * X))
         def _():
             alone.after_x(t // X - 2)
             alone.z_copy(t // X - 2).start()

time: 69.5 us -> 68.9 us (level)
  no operation moved by 1% of the time
where the time goes in v4:
time: 68.9 us; the launch traced here: 68.8 us
  Pallas kernels  67 us (97%)
  local copies, waits for them, and re-layouts  1.23 us (2%)
    pallas_call x1, Pallas kernels, shards(): pl.pallas_call(kernel, out_shape=(jax.ShapeDtypeStruct((examples, LANES),...  67 us

profile of v4, /device:TPU:1, one launch (start us, length us, event | category | flops | bytes accessed | tf_op | source)
XLA Modules:
  0.0 68.8 jit_solution(5887779960383890832)
XLA Ops:
  0.6 67.0 %features_and_scores.1 = (f32[64,128]{1,0:T(8,128)S(1)}, f32[64,57]{1,0:T(8,128)S(1)}) custom-call(f32[64,4096]{1,0:T(8,128)} %g_in.1, f32[32,128]{1,0:T(8,128)} %bitcast.6, f32[32,128]{1,0:T(8,128)} %bitcast.7, s32[32,128]{1,0:T(8,128)} %bitcast.8, s32[64,128]{1,0:T(8,128)} %bitcast.5, s32[2,128]{1,0:T(2,128)} %bitcast.9), custom_call_target="tpu_custom_call" | custom-call | tf_op jit(solution)/shard_map/features_and_scores/pallas_call | solution.py:417
  67.6 0.6 copy.10
  68.2 0.6 copy.11

commit v5 on v4

--- a/solution.py
+++ b/solution.py
@@ -114,11 +114,11 @@
     u_own, u_both, g_other, seeds,
     part_a, chip_a, sum_a, cols_a, rows_a, got_a,
     part_b, chip_b, sum_b, cols_b, rows_b, got_b,
-    ybuf, blocks, send1, recv1, planes, scored,
+    ybuf, blocks, send1, recv1, planes, norm1, norm_recv, norm_planes, scored,
     gs, gr,
     cs_a, cr_a, xs_a, xr_a, zs_a, zr_a,
     cs_b, cr_b, xs_b, xr_b, zs_b, zr_b,
-    ys, yr, s1s, s1r, s2s, s2r, o1s, o1r,
+    ys, yr, s1s, s1r, s2s, s2r, n1s, n1r, n2s, n2r, o1s, o1r,
 ):
     me, y = lax.axis_index("param"), lax.axis_index("ex")
     x, z, c = me // (Z * C), (me // C) % Z, me % C
@@ -313,40 +313,52 @@
 
     products = contract(total, every)
     squares = contract(jnp.ones((8, LANES), F32), every * every)
-    send1[...] = jnp.zeros_like(send1)
+    for h in range(2):
+        norm1[h : h + 1, :] = squares[:1, h * LANES : (h + 1) * LANES]
     for j in range(XC):
-        send1[j, :, : Y * examples] = products[j * Z : (j + 1) * Z, :]
-        for h in range(2):
-            send1[j, h : h + 1, Y * examples :] = squares[:1, h * LANES : (h + 1) * LANES]
-
-    def send1_copy(d):
+        send1[j] = products[j * Z : (j + 1) * Z, :]
+
+    def send1_copies(d):
         to = (xc + d) % XC
-        return send(send1.at[to], recv1.at[d - 1], s1s.at[d - 1], s1r.at[d - 1], at_xc(to))
-
-    for d in range(1, XC):
-        send1_copy(d).start()
+        return (
+            send(norm1, norm_recv.at[d - 1], n1s.at[d - 1], n1r.at[d - 1], at_xc(to)),
+            send(send1.at[to], recv1.at[d - 1], s1s.at[d - 1], s1r.at[d - 1], at_xc(to)),
+        )
+
+    for d in range(1, XC):
+        for copy in send1_copies(d):
+            copy.start()
     for d in range(1, Y):
         y_copy(d).wait_send()
-    block = send1[xc]
-    for d in range(1, XC):
-        send1_copy(d).wait_recv()
-        block = block + recv1[d - 1]
+    block, norm = send1[xc], norm1[...]
+    for d in range(1, XC):
+        for copy in send1_copies(d):
+            copy.wait_recv()
+        block, norm = block + recv1[d - 1], norm + norm_recv[d - 1]
     planes[z] = block
-
-    def plane_copy(d):
-        return send(planes.at[z], planes.at[z], s2s.at[d - 1], s2r.at[d - 1], at(x, (z + d) % Z, c))
+    norm_planes[z] = norm
+
+    def plane_copies(d):
+        to = at(x, (z + d) % Z, c)
+        return (
+            send(norm_planes.at[z], norm_planes.at[z], n2s.at[d - 1], n2r.at[d - 1], to),
+            send(planes.at[z], planes.at[z], s2s.at[d - 1], s2r.at[d - 1], to),
+        )
 
     for d in FARTHEST_FIRST:
-        plane_copy(d).start()
-    for d in range(1, XC):
-        send1_copy(d).wait_send()
+        for copy in plane_copies(d):
+            copy.start()
+    for d in range(1, XC):
+        for copy in send1_copies(d):
+            copy.wait_send()
     for d in range(1, Z):
-        plane_copy(d).wait_recv()
-    block = planes[0]
+        for copy in plane_copies(d):
+            copy.wait_recv()
+    block, norm = planes[0], norm_planes[0]
     for j in range(1, Z):
-        block = block + planes[j]
-
-    root_mean = jnp.sqrt(block[:2, Y * examples :] / features + 1e-06)
+        block, norm = block + planes[j], norm + norm_planes[j]
+
+    root_mean = jnp.sqrt(norm / features + 1e-06)
     example = y * examples + xc * Z + lax.broadcasted_iota(jnp.int32, (Z, LANES), 0)
     lane = lax.broadcasted_iota(jnp.int32, (Z, LANES), 1)
     labels = lax.broadcasted_iota(jnp.int32, (LANES, LANES), 0)
@@ -367,7 +379,8 @@
     for d in range(1, XC):
         score_copy(d).start()
     for d in range(1, Z):
-        plane_copy(d).wait_send()
+        for copy in plane_copies(d):
+            copy.wait_send()
 
     here = y * examples + lax.broadcasted_iota(jnp.int32, (examples, LANES), 0)
     lane = lax.broadcasted_iota(jnp.int32, (examples, LANES), 1)
@@ -390,7 +403,7 @@
         examples, params = gradients.shape
         rows = (-1, LANES)
         dma, vmem = pltpu.SemaphoreType.DMA, pltpu.VMEM
-        wide = (Y * examples) + LANES
+        wide = Y * examples
 
         def buffers(groups, rows):
             block = (rows, LANES)
@@ -436,11 +449,16 @@
                 vmem((XC, Z, wide), F32),
                 vmem((XC - 1, Z, wide), F32),
                 vmem((Z, Z, wide), F32),
+                vmem((2, LANES), F32),
+                vmem((XC - 1, 2, LANES), F32),
+                vmem((Z, 2, LANES), F32),
                 vmem((XC, Z, LANES), F32),
                 dma((1,)), dma((1,)),
                 *semaphores(ALONE),
                 *semaphores(Z - ALONE),
                 dma((Y - 1,)), dma((Y - 1,)),
+                dma((XC - 1,)), dma((XC - 1,)),
+                dma((Z - 1,)), dma((Z - 1,)),
                 dma((XC - 1,)), dma((XC - 1,)),
                 dma((Z - 1,)), dma((Z - 1,)),
                 dma((XC - 1,)), dma((XC - 1,)),

time: 68.9 us -> 69.1 us (level)
  no operation moved by 1% of the time
where the time goes in v5:
time: 69.1 us; the launch traced here: 69 us
  Pallas kernels  67.2 us (97%)
  local copies, waits for them, and re-layouts  1.23 us (2%)
    pallas_call x1, Pallas kernels, shards(): pl.pallas_call(kernel, out_shape=(jax.ShapeDtypeStruct((examples, LANES),...  67.2 us

profile of v5, /device:TPU:1, one launch (start us, length us, event | category | flops | bytes accessed | tf_op | source)
XLA Modules:
  0.0 69.0 jit_solution(17090233527868139286)
XLA Ops:
  0.6 67.2 %features_and_scores.1 = (f32[64,128]{1,0:T(8,128)S(1)}, f32[64,57]{1,0:T(8,128)S(1)}) custom-call(f32[64,4096]{1,0:T(8,128)} %g_in.1, f32[32,128]{1,0:T(8,128)} %bitcast.6, f32[32,128]{1,0:T(8,128)} %bitcast.7, s32[32,128]{1,0:T(8,128)} %bitcast.8, s32[64,128]{1,0:T(8,128)} %bitcast.5, s32[2,128]{1,0:T(2,128)} %bitcast.9), custom_call_target="tpu_custom_call" | custom-call | tf_op jit(solution)/shard_map/features_and_scores/pallas_call | solution.py:430
  67.8 0.6 copy.10
  68.4 0.6 copy.11
